TPU v7x, 128 devices: a whole 4x4x4 slice. The times are simulated.
128 devices in a mesh: row: 8 (over y, z_hi), col: 16 (over x, z_lo, core).
Axes of the slice: x: 4, y: 4, z: 4 (z_hi: 2, z_lo: 2; z = z_hi * 2 + z_lo), core: 2. Of those that a mesh axis runs over, the one named last changes fastest.
Arguments:
- costs: bfloat16 [256, 2048, 128], P('row', 'col'), may hold values from 0 to 63, as said below
- p_small: int32 [1], replicated, may hold values from 4 to 16
- p_large: int32 [1], replicated, may hold values from 32 to 96
Outputs:
- left_view: bfloat16 [256, 2048, 128], P('row', 'col')
- right_view: bfloat16 [256, 2048, 128], P('row', 'col')
Inputs may be any that keep to these rules, and one draw needn't show every extreme that they name: `costs`: whole numbers.
All inputs are finite; a program needn't handle non-finite values.
Results may differ from a plain program's by a relative error of at most 0.001.
Values may be sent and summed in bfloat16 or wider, within the bound.
A program may use at most 64 MiB of HBM per device.

v0:
```python
import jax
import jax.numpy as jnp
from jax import lax
from jax.experimental import pallas as pl
from jax.experimental.pallas import tpu as pltpu
from jax.sharding import PartitionSpec as P

MESH = pl.DeviceIdType.MESH
F32 = jnp.float32
BF16 = jnp.bfloat16
FAR = 1.0e9

TH, TW, D = 32, 128, 128
NJ = 16


def nt_dot(a, b):
    return lax.dot_general(a, b, (((1,), (1,)), ((), ())), preferred_element_type=F32)


def to_slab(ref, base, v):
    for a in range(NJ):
        ref[pl.ds(base + (a % 2) * 64 + a // 2, 8, stride=8), :] = v[8 * a : 8 * a + 8]


def from_slab(ref, base):
    return [ref[pl.ds(base + (a % 2) * 64 + a // 2, 8, stride=8), :] for a in range(NJ)]


def step(u, c, q1, q2, first, last):
    low = jnp.where(first, FAR, pltpu.roll(u[NJ - 1], 1, 0))
    high = jnp.where(last, FAR, pltpu.roll(u[0], 7, 0))
    sides = []
    for j in range(NJ):
        a = u[j - 1] if j else low
        b = u[j + 1] if j < NJ - 1 else high
        sides.append(jnp.minimum(a, b))
    parts = [sides[j] for j in range(NJ) if j % 4 in (1, 2)]
    while len(parts) > 1:
        parts = [jnp.minimum(parts[i], parts[i + 1]) for i in range(0, len(parts), 2)]
    m = parts[0]
    for s in (4, 2, 1):
        m = jnp.minimum(m, pltpu.roll(m, s, 0))
    jump = m + q2
    out = [
        jnp.minimum(jnp.minimum(u[j], sides[j] + q1), jump) + c[8 * j : 8 * j + 8]
        for j in range(NJ)
    ]
    return out, m


def kernel(
    small_ref, large_ref, costs_ref, left_ref, right_ref,
    c_h, c_v, path_h, low_h, path_v, low_v, acc, beyond,
    out_h, in_h, out_v, in_v, send_h, recv_h, send_v, recv_v, send_b, recv_b,
):
    row, col = lax.axis_index("row"), lax.axis_index("col")
    rows, cols = lax.axis_size("row"), lax.axis_size("col")

    barrier = pltpu.get_barrier_semaphore()
    partners = [
        (col > 0, row, col - 1),
        (col < cols - 1, row, col + 1),
        (row > 0, row - 1, col),
        (row < rows - 1, row + 1, col),
    ]
    for there, r, c in partners:

        @pl.when(there)
        def _(r=r, c=c):
            pl.semaphore_signal(barrier, inc=1, device_id=(r, c), device_id_type=MESH)

    missing = sum(jnp.where(there, 0, 1) for there, _, _ in partners)
    pl.semaphore_wait(barrier, 4 - missing)

    q1 = jnp.full((8, 128), small_ref[0].astype(F32))
    q2 = jnp.full((8, 128), large_ref[0].astype(F32))
    sub = lax.broadcasted_iota(jnp.int32, (8, 128), 0)
    lane = lax.broadcasted_iota(jnp.int32, (8, 128), 1)
    first, last = sub == 0, sub == 7
    r0 = lax.broadcasted_iota(jnp.int32, (D, D), 0)
    r1 = lax.broadcasted_iota(jnp.int32, (D, D), 1)
    perm = (r1 == (r0 % 8) * 16 + r0 // 8).astype(F32).astype(BF16)

    @pl.loop(0, TH)
    def _(y):
        acc[pl.ds(pl.multiple_of(y * TW, TW), TW), :] = costs_ref[y].astype(F32)

    @pl.loop(0, TW // 4)
    def _(g):
        for k in range(4):
            x = 4 * g + k
            a = acc[pl.ds(x, TH, stride=TW), :]
            if k % 2:
                a = a.astype(BF16)
                c_h[pl.ds(pl.multiple_of(x * D, D), D), :] = nt_dot(perm, jnp.concatenate([a] * 4, axis=0))
            else:
                to_slab(c_h, x * D, jnp.transpose(jnp.concatenate([a] * 4, axis=0)))

    def columns():
        @pl.loop(0, TH, unroll=4)
        def _(y):
            c_v[pl.ds(pl.multiple_of(y * D, D), D), :] = nt_dot(perm, costs_ref[y])

    def h_copy(way):
        return pltpu.make_async_remote_copy(
            out_h.at[way], in_h.at[way], send_h.at[way], recv_h.at[way],
            device_id=(row, col + 1 - 2 * way), device_id_type=MESH,
        )

    def v_copy(way):
        return pltpu.make_async_remote_copy(
            out_v.at[way], in_v.at[way], send_v.at[way], recv_v.at[way],
            device_id=(row + 1 - 2 * way, col), device_id_type=MESH,
        )

    def along_row(way):
        at = jnp.where(way == 0, col, cols - 1 - col)

        @pl.when(at == 0)
        def _():
            in_h[way] = jnp.zeros((32, 128), BF16)

        @pl.when(at > 0)
        def _():
            h_copy(way).wait_recv()

        got = in_h[way].astype(F32)
        got = [got[8 * i : 8 * i + 8] for i in range(4)]
        turned = [[v] + [pltpu.roll(v, 32 * k, 1) for k in (1, 2, 3)] for v in got]
        u = []
        for g in range(4):
            for i in range(4):
                v = turned[i][-g % 4]
                for h in range(1, 4):
                    v = jnp.where(lane >= 32 * h, turned[i][(h - g) % 4], v)
                u.append(v)

        def body(t, carry):
            u, _ = carry
            x = jnp.where(way == 0, t, TW - 1 - t)
            at = pl.ds(pl.multiple_of(x * D, D), D)
            u, m = step(u, c_h[at, :], q1, q2, first, last)
            mine = lane // 32 == x % 4
            base = pl.multiple_of(x // 4 * D, D)
            for j in range(NJ):
                pltpu.store(path_h.at[way, pl.ds(base + 8 * j, 8), :], u[j], mask=mine)
            pltpu.store(low_h.at[way, x // 4], m, mask=mine)
            return u, m

        u, m = lax.fori_loop(0, TW, body, (u, jnp.zeros((8, 128), F32)), unroll=4)

        @pl.when(at < cols - 1)
        def _():
            packed = []
            for i in range(4):
                v = u[i]
                for g in range(1, 4):
                    v = jnp.where(lane >= 32 * g, u[4 * g + i], v)
                packed.append(v - m)
            out_h[way] = jnp.concatenate(packed, axis=0).astype(BF16)
            h_copy(way).start()

    def along_col(way):
        at = jnp.where(way == 0, row, rows - 1 - row)

        @pl.when(at == 0)
        def _():
            in_v[way] = jnp.zeros((D, 128), BF16)

        @pl.when(at > 0)
        def _():
            v_copy(way).wait_recv()

        got = in_v[way].astype(F32)
        u = [got[8 * j : 8 * j + 8] for j in range(NJ)]

        def body(t, carry):
            u, _ = carry
            y = jnp.where(way == 0, t, TH - 1 - t)
            at = pl.ds(pl.multiple_of(y * D, D), D)
            u, m = step(u, c_v[at, :], q1, q2, first, last)
            path_v[way, at, :] = jnp.concatenate(u, axis=0)
            low_v[way, y] = m
            return u, m

        u, m = lax.fori_loop(0, TH, body, (u, jnp.zeros((8, 128), F32)), unroll=2)

        @pl.when(at < rows - 1)
        def _():
            out_v[way] = jnp.concatenate([v - m for v in u], axis=0).astype(BF16)
            v_copy(way).start()

    near = jnp.minimum(col, cols - 1 - col)
    h_one = jnp.where(col * 2 < cols, 0, 1)
    v_near = jnp.minimum(row, rows - 1 - row)
    v_one = jnp.where(row * 2 < rows, 0, 1)
    before = (near * 3) // 4
    until = before + ((cols - 2 - 2 * near) * 3) // 4

    def add_columns():
        @pl.loop(0, TH, unroll=2)
        def _(y):
            base = pl.multiple_of(y * D, D)
            low = low_v[0, y] + low_v[1, y]
            both = zip(from_slab(path_v.at[0], base), from_slab(path_v.at[1], base))
            acc[pl.ds(base, TW), :] = jnp.transpose(jnp.concatenate([a + b - low for a, b in both], axis=0))

    def add_rows(way):
        @pl.loop(0, TW // 4, unroll=2)
        def _(g):
            low = low_h[way, g]
            v = [a - low for a in from_slab(path_h.at[way], pl.multiple_of(g * D, D))]
            v = jnp.transpose(jnp.concatenate(v, axis=0))
            for k in range(4):
                at = pl.ds(4 * g + k, TH, stride=TW)
                acc[at, :] = acc[at, :] + v[TH * k : TH * (k + 1)]

    v_late = rows - 1 - v_near >= until

    @pl.loop(0, 9)
    def _(p):
        part, which = p // 3, p % 3
        slot = jnp.where(which == 0, v_near, rows - 1 - v_near)
        v_part = jnp.where(slot < before, 0, jnp.where(slot < until, 1, 2))

        @pl.when(p == jnp.where(near < 2, 3, 0))
        def _():
            columns()

        @pl.when(p == jnp.where(v_late, 8, 5))
        def _():
            add_columns()
            add_rows(h_one)

        @pl.when(jnp.logical_and(which == 2, part < 2))
        def _():
            along_row(jnp.where(part == 0, h_one, 1 - h_one))

        @pl.when(jnp.logical_and(which < 2, v_part == part))
        def _():
            along_col(jnp.where(which == 0, v_one, 1 - v_one))

    add_rows(1 - h_one)

    CH = TH // 4

    def next_tile(q):
        at = pl.ds(q * CH, CH)
        return pltpu.make_async_remote_copy(
            left_ref.at[at], beyond.at[at], send_b.at[q], recv_b.at[q],
            device_id=(row, col - 1), device_id_type=MESH,
        )

    @pl.loop(0, 4)
    def _(q):
        @pl.loop(q * CH, (q + 1) * CH)
        def _(y):
            left_ref[y] = (acc[pl.ds(pl.multiple_of(y * TW, TW), TW), :] * (1.0 / 64.0)).astype(BF16)

        @pl.when(col > 0)
        def _():
            next_tile(q).start()

    @pl.when(col == cols - 1)
    def _():
        beyond[...] = jnp.zeros((TH, TW, D), BF16)

    @pl.loop(0, 4)
    def _(q):
        @pl.when(col < cols - 1)
        def _():
            next_tile(q).wait_recv()

        @pl.loop(q * CH, (q + 1) * CH)
        def _(y):
            v = jnp.concatenate([left_ref[y], beyond[y]], axis=0).astype(F32)
            for bit, size in ((64, 192), (32, 160), (16, 144), (8, 136)):
                d = lax.broadcasted_iota(jnp.int32, (size, D), 1)
                v = jnp.where((d & bit) != 0, v[bit : bit + size], v[:size])
            d = lax.broadcasted_iota(jnp.int32, (136, D), 1)
            for bit in (4, 2, 1):
                v = jnp.where((d & bit) != 0, pltpu.roll(v, 136 - bit, 0), v)
            right_ref[y] = v[:TW].astype(BF16)

    for way in (0, 1):
        at_h = col if way == 0 else cols - 1 - col
        at_v = row if way == 0 else rows - 1 - row

        @pl.when(at_h < cols - 1)
        def _(way=way):
            h_copy(way).wait_send()

        @pl.when(at_v < rows - 1)
        def _(way=way):
            v_copy(way).wait_send()

    @pl.when(col > 0)
    def _():
        for q in range(4):
            next_tile(q).wait_send()


def shards(costs, p_small, p_large):
    tile = jax.ShapeDtypeStruct(costs.shape, BF16)
    return pl.pallas_call(
        kernel,
        out_shape=(tile, tile),
        in_specs=[
            pl.BlockSpec(memory_space=pltpu.SMEM),
            pl.BlockSpec(memory_space=pltpu.SMEM),
            pl.BlockSpec(memory_space=pltpu.VMEM),
        ],
        out_specs=(pl.BlockSpec(memory_space=pltpu.VMEM), pl.BlockSpec(memory_space=pltpu.VMEM)),
        scratch_shapes=[
            pltpu.VMEM((TW * D, 128), F32),
            pltpu.VMEM((TH * D, 128), F32),
            pltpu.VMEM((2, TW // 4 * D, 128), F32),
            pltpu.VMEM((2, TW // 4, 8, 128), F32),
            pltpu.VMEM((2, TH * D, 128), F32),
            pltpu.VMEM((2, TH, 8, 128), F32),
            pltpu.VMEM((TH * TW, D), F32),
            pltpu.VMEM((TH, TW, D), BF16),
            pltpu.VMEM((2, 32, 128), BF16),
            pltpu.VMEM((2, 32, 128), BF16),
            pltpu.VMEM((2, D, 128), BF16),
            pltpu.VMEM((2, D, 128), BF16),
            pltpu.SemaphoreType.DMA((2,)),
            pltpu.SemaphoreType.DMA((2,)),
            pltpu.SemaphoreType.DMA((2,)),
            pltpu.SemaphoreType.DMA((2,)),
            pltpu.SemaphoreType.DMA((4,)),
            pltpu.SemaphoreType.DMA((4,)),
        ],
        compiler_params=pltpu.CompilerParams(collective_id=0, has_side_effects=True),
        name="sgm",
    )(p_small, p_large, costs)


def solution(mesh):
    placed = (P("row", "col", None), P(), P())
    return jax.shard_map(
        shards,
        mesh=mesh,
        in_specs=placed,
        out_specs=(P("row", "col", None), P("row", "col", None)),
        check_vma=False,
    )
```

profile of v0, /device:TPU:23, one launch (start us, length us, event | category | flops | bytes accessed | tf_op | source)
XLA Modules:
  0.0 97.1 jit_solution(14681289250405616344)
XLA Ops:
  1.9 91.8 %sgm.1 = (bf16[32,128,128]{2,1,0:T(8,128)(2,1)}, bf16[32,128,128]{2,1,0:T(8,128)(2,1)}) custom-call(s32[1]{0:T(128)S(6)} %copy.7.small_ref, s32[1]{0:T(128)S(6)} %copy.8.large_ref, bf16[32,128,128]{2,1,0:T(8,128)(2,1)} %costs_ref.1), custom_call_target="tpu_custom_call" | custom-call | tf_op jit(solution)/shard_map/sgm/pallas_call | solution.py:306
  93.7 0.0 copy-start
  93.7 2.4 %copy.9 = bf16[32,128,128]{2,1,0:T(8,128)(2,1)} copy(bf16[32,128,128]{2,1,0:T(8,128)(2,1)} %get-tuple-element.4) | data formatting | bytes 2097152
  96.1 0.0 copy-done
  96.1 1.0 copy.10
Async XLA Ops:
  93.7 2.4 %copy-start = (bf16[32,128,128]{2,1,0:T(8,128)(2,1)S(1)}, bf16[32,128,128]{2,1,0:T(8,128)(2,1)}, u32[]{:S(2)}) copy-start(bf16[32,128,128]{2,1,0:T(8,128)(2,1)} %get-tuple-element.5) | copy-start | bytes 3145732
where the time goes:
time: 97.3 us; the launch traced here: 97.1 us
  Pallas kernels  91.8 us (94%)
  local copies, waits for them, and re-layouts  3.37 us (3%)
  between operations  1.94 us (2%)
    pallas_call x1, Pallas kernels, shards(): pl.pallas_call(kernel, out_shape=(tile, tile), in_specs=[pl.BlockSpec(mem...  91.8 us
    unnamed x4, local copies, waits for them, and re-layouts  3.37 us

commit v1 on v0

--- a/solution.py
+++ b/solution.py
@@ -12,6 +12,8 @@
 
 TH, TW, D = 32, 128, 128
 NJ = 16
+FOLD = 80
+PITCH = 136
 
 
 def nt_dot(a, b):
@@ -50,9 +52,9 @@
 
 
 def kernel(
-    small_ref, large_ref, costs_ref, left_ref, right_ref,
+    small_ref, large_ref, costs_ref, left_out, right_out, left_ref, right_ref, folded,
     c_h, c_v, path_h, low_h, path_v, low_v, acc, beyond,
-    out_h, in_h, out_v, in_v, send_h, recv_h, send_v, recv_v, send_b, recv_b,
+    out_h, in_h, out_v, in_v, send_h, recv_h, send_v, recv_v, send_b, recv_b, done_l, done_r,
 ):
     row, col = lax.axis_index("row"), lax.axis_index("col")
     rows, cols = lax.axis_size("row"), lax.axis_size("col")
@@ -84,13 +86,13 @@
 
     @pl.loop(0, TH)
     def _(y):
-        acc[pl.ds(pl.multiple_of(y * TW, TW), TW), :] = costs_ref[y].astype(F32)
+        acc[pl.ds(pl.multiple_of(y * PITCH, 8), TW), :] = costs_ref[y].astype(F32)
 
     @pl.loop(0, TW // 4)
     def _(g):
         for k in range(4):
             x = 4 * g + k
-            a = acc[pl.ds(x, TH, stride=TW), :]
+            a = acc[pl.ds(x, TH, stride=PITCH), :]
             if k % 2:
                 a = a.astype(BF16)
                 c_h[pl.ds(pl.multiple_of(x * D, D), D), :] = nt_dot(perm, jnp.concatenate([a] * 4, axis=0))
@@ -204,7 +206,7 @@
             base = pl.multiple_of(y * D, D)
             low = low_v[0, y] + low_v[1, y]
             both = zip(from_slab(path_v.at[0], base), from_slab(path_v.at[1], base))
-            acc[pl.ds(base, TW), :] = jnp.transpose(jnp.concatenate([a + b - low for a, b in both], axis=0))
+            acc[pl.ds(pl.multiple_of(y * PITCH, 8), TW), :] = jnp.transpose(jnp.concatenate([a + b - low for a, b in both], axis=0))
 
     def add_rows(way):
         @pl.loop(0, TW // 4, unroll=2)
@@ -213,7 +215,7 @@
             v = [a - low for a in from_slab(path_h.at[way], pl.multiple_of(g * D, D))]
             v = jnp.transpose(jnp.concatenate(v, axis=0))
             for k in range(4):
-                at = pl.ds(4 * g + k, TH, stride=TW)
+                at = pl.ds(4 * g + k, TH, stride=PITCH)
                 acc[at, :] = acc[at, :] + v[TH * k : TH * (k + 1)]
 
     v_late = rows - 1 - v_near >= until
@@ -248,23 +250,35 @@
     def next_tile(q):
         at = pl.ds(q * CH, CH)
         return pltpu.make_async_remote_copy(
-            left_ref.at[at], beyond.at[at], send_b.at[q], recv_b.at[q],
+            folded.at[at], beyond.at[at], send_b.at[q], recv_b.at[q],
             device_id=(row, col - 1), device_id_type=MESH,
         )
+
+    def write(src, dst, sem, q):
+        at = pl.ds(q * CH, CH)
+        return pltpu.make_async_copy(src.at[at], dst.at[at], sem.at[q])
+
+    lane32 = lax.broadcasted_iota(jnp.int32, (32, D), 1)
 
     @pl.loop(0, 4)
     def _(q):
         @pl.loop(q * CH, (q + 1) * CH)
         def _(y):
-            left_ref[y] = (acc[pl.ds(pl.multiple_of(y * TW, TW), TW), :] * (1.0 / 64.0)).astype(BF16)
+            v = acc[pl.ds(pl.multiple_of(y * PITCH, 8), TW), :] * (1.0 / 64.0)
+            left_ref[y] = v.astype(BF16)
+            one = jnp.where(lane32 < 32, pltpu.roll(v[96:], 32, 1), v[32:64])
+            two = jnp.where(lane32[:16] < 64, pltpu.roll(v[80:96], 64, 1), v[64:80])
+            folded[y] = jnp.concatenate([v[:32], one, two], axis=0).astype(BF16)
 
         @pl.when(col > 0)
         def _():
             next_tile(q).start()
+
+        write(left_ref, left_out, done_l, q).start()
 
     @pl.when(col == cols - 1)
     def _():
-        beyond[...] = jnp.zeros((TH, TW, D), BF16)
+        beyond[...] = jnp.zeros((TH, FOLD, D), BF16)
 
     @pl.loop(0, 4)
     def _(q):
@@ -274,7 +288,10 @@
 
         @pl.loop(q * CH, (q + 1) * CH)
         def _(y):
-            v = jnp.concatenate([left_ref[y], beyond[y]], axis=0).astype(F32)
+            f = beyond[y].astype(F32)
+            v = jnp.concatenate(
+                [left_ref[y].astype(F32), f, pltpu.roll(f[64:80], 64, 1), pltpu.roll(f[32:64], 96, 1)], axis=0
+            )
             for bit, size in ((64, 192), (32, 160), (16, 144), (8, 136)):
                 d = lax.broadcasted_iota(jnp.int32, (size, D), 1)
                 v = jnp.where((d & bit) != 0, v[bit : bit + size], v[:size])
@@ -282,6 +299,12 @@
             for bit in (4, 2, 1):
                 v = jnp.where((d & bit) != 0, pltpu.roll(v, 136 - bit, 0), v)
             right_ref[y] = v[:TW].astype(BF16)
+
+        write(right_ref, right_out, done_r, q).start()
+
+    for q in range(4):
+        write(left_ref, left_out, done_l, q).wait()
+        write(right_ref, right_out, done_r, q).wait()
 
     for way in (0, 1):
         at_h = col if way == 0 else cols - 1 - col
@@ -311,16 +334,19 @@
             pl.BlockSpec(memory_space=pltpu.SMEM),
             pl.BlockSpec(memory_space=pltpu.VMEM),
         ],
-        out_specs=(pl.BlockSpec(memory_space=pltpu.VMEM), pl.BlockSpec(memory_space=pltpu.VMEM)),
+        out_specs=(pl.BlockSpec(memory_space=pl.ANY), pl.BlockSpec(memory_space=pl.ANY)),
         scratch_shapes=[
+            pltpu.VMEM((TH, TW, D), BF16),
+            pltpu.VMEM((TH, TW, D), BF16),
+            pltpu.VMEM((TH, FOLD, D), BF16),
             pltpu.VMEM((TW * D, 128), F32),
             pltpu.VMEM((TH * D, 128), F32),
             pltpu.VMEM((2, TW // 4 * D, 128), F32),
             pltpu.VMEM((2, TW // 4, 8, 128), F32),
             pltpu.VMEM((2, TH * D, 128), F32),
             pltpu.VMEM((2, TH, 8, 128), F32),
-            pltpu.VMEM((TH * TW, D), F32),
-            pltpu.VMEM((TH, TW, D), BF16),
+            pltpu.VMEM((TH * PITCH, D), F32),
+            pltpu.VMEM((TH, FOLD, D), BF16),
             pltpu.VMEM((2, 32, 128), BF16),
             pltpu.VMEM((2, 32, 128), BF16),
             pltpu.VMEM((2, D, 128), BF16),
@@ -331,6 +357,8 @@
             pltpu.SemaphoreType.DMA((2,)),
             pltpu.SemaphoreType.DMA((4,)),
             pltpu.SemaphoreType.DMA((4,)),
+            pltpu.SemaphoreType.DMA((4,)),
+            pltpu.SemaphoreType.DMA((4,)),
         ],
         compiler_params=pltpu.CompilerParams(collective_id=0, has_side_effects=True),
         name="sgm",

time: 97.3 us -> 90.5 us (0.930)
  Pallas kernels: 91.8 us -> 85 us
    pallas_call x1, Pallas kernels: 91.8 us -> 85 us  [shards(): pl.pallas_call(kernel, out_shape=(tile, tile), in_specs=[pl.BlockSpec(mem...]
where the time goes in v1:
time: 90.5 us; the launch traced here: 90.3 us
  Pallas kernels  85 us (94%)
  local copies, waits for them, and re-layouts  3.37 us (4%)
  between operations  1.94 us (2%)
    pallas_call x1, Pallas kernels, shards(): pl.pallas_call(kernel, out_shape=(tile, tile), in_specs=[pl.BlockSpec(mem...  85 us
    unnamed x4, local copies, waits for them, and re-layouts  3.37 us

profile of v1, /device:TPU:23, one launch (start us, length us, event | category | flops | bytes accessed | tf_op | source)
XLA Modules:
  0.0 90.3 jit_solution(8750937232462566901)
XLA Ops:
  1.9 85.0 %sgm.1 = (bf16[32,128,128]{2,1,0:T(8,128)(2,1)}, bf16[32,128,128]{2,1,0:T(8,128)(2,1)}) custom-call(s32[1]{0:T(128)S(6)} %copy.7.small_ref, s32[1]{0:T(128)S(6)} %copy.8.large_ref, bf16[32,128,128]{2,1,0:T(8,128)(2,1)} %costs_ref.1), custom_call_target="tpu_custom_call" | custom-call | tf_op jit(solution)/shard_map/sgm/pallas_call | solution.py:329
  86.9 0.0 copy-start
  86.9 2.4 %copy.9 = bf16[32,128,128]{2,1,0:T(8,128)(2,1)} copy(bf16[32,128,128]{2,1,0:T(8,128)(2,1)} %get-tuple-element.4) | data formatting | bytes 2097152
  89.3 0.0 copy-done
  89.3 1.0 %copy.10 = bf16[32,128,128]{2,1,0:T(8,128)(2,1)} copy(bf16[32,128,128]{2,1,0:T(8,128)(2,1)S(1)} %copy-done) | data formatting | bytes 2097152
Async XLA Ops:
  86.9 2.4 %copy-start = (bf16[32,128,128]{2,1,0:T(8,128)(2,1)S(1)}, bf16[32,128,128]{2,1,0:T(8,128)(2,1)}, u32[]{:S(2)}) copy-start(bf16[32,128,128]{2,1,0:T(8,128)(2,1)} %get-tuple-element.5) | copy-start | bytes 3145732
